TPU v7x, 32 devices: a whole 2x2x4 slice. The times are simulated.
32 devices in a mesh: row: 1, col: 16 (over z, y, core), seg: 2 (over x).
Axes of the slice: x: 2, y: 2, z: 4, core: 2. Of those that a mesh axis runs over, the one named last changes fastest.
Arguments:
- traces: bfloat16 [8, 128, 1024], P('seg', ('row', 'col')), may hold values from -600 to 600, as said below
- valid: int32 [8, 128], P('seg', ('row', 'col')), may hold values 0 or 1
Outputs:
- correlation: float32 [33, 1, 128, 128], P(None, None, ('col', 'seg'), 'row')
Inputs may be any that keep to these rules, and one draw needn't show every extreme that they name: `traces`: samples of a common wavefield delayed by up to 32 samples per station plus noise, scaled per station.
All inputs are finite; a program needn't handle non-finite values. No bound on the sum of `valid` on one device may be relied on, other than what follows from the above.
Results may differ from a plain program's by a relative error of at most 0.002.
Values may be sent and summed in bfloat16 or wider, within the bound.
No kernel may reach another device: no remote copies, remote signals or barrier semaphores. Data moves between devices by JAX's collectives and lax.ppermute only.
A program may use at most 64 MiB of HBM per device.

v0:
```python
import math
import jax
import jax.numpy as jnp
from jax import lax
from jax.sharding import PartitionSpec as P

MAXLAG = 16
LAGSET = 3


def make_tables(length, max_shift):
    bins = jnp.arange(length // 2, dtype=jnp.int32)
    samples = jnp.arange(length, dtype=jnp.int32)
    product = samples[:, None] * bins[None, :] % length
    angle = 2.0 * math.pi / length * product.astype(jnp.float32)
    dft_table = jnp.concatenate([jnp.cos(angle), -jnp.sin(angle)], axis=1).astype(jnp.bfloat16)
    shifts = jnp.arange(2 * max_shift + 1, dtype=jnp.int32) - max_shift
    lag_prod = shifts[:, None] * bins[None, :] % length
    lag_angle = 2.0 * math.pi / length * lag_prod.astype(jnp.float32)
    return (dft_table, jnp.cos(lag_angle), jnp.sin(lag_angle))


def whiten(traces, valid, dft_table):
    length = traces.shape[2]
    half = length // 2
    flat = traces.reshape(-1, length)
    spectrum = jnp.dot(flat, dft_table, preferred_element_type=jnp.float32)
    spectrum = spectrum.reshape(traces.shape[0], traces.shape[1], length)
    real_part = spectrum[..., :half]
    imag_part = spectrum[..., half:]
    power = real_part * real_part + imag_part * imag_part
    level = jnp.mean(power, axis=-1, keepdims=True)
    factor = lax.rsqrt(power + 0.1 * level + 1e-05) * valid[..., None].astype(jnp.float32)
    return jnp.concatenate([real_part * factor, imag_part * factor], axis=-1).astype(jnp.bfloat16)


def lag_sums(first_set, second_set, cosines, sines, group_size):
    half = first_set.shape[2] // 2
    lag_count = cosines.shape[0]
    real_part = second_set[..., :half].astype(jnp.float32)
    imag_part = second_set[..., half:].astype(jnp.float32)

    def one_group(group):
        cosine = lax.dynamic_slice_in_dim(cosines, group * group_size, group_size, 0)[
            :, None, None, :
        ]
        sine = lax.dynamic_slice_in_dim(sines, group * group_size, group_size, 0)[:, None, None, :]
        first = real_part[None] * cosine + imag_part[None] * sine
        second = imag_part[None] * cosine - real_part[None] * sine
        rotated = jnp.concatenate([first, second], axis=-1).astype(jnp.bfloat16)
        return jnp.einsum("gsbk,sak->gba", rotated, first_set, preferred_element_type=jnp.float32)

    result = lax.map(one_group, jnp.arange(lag_count // group_size, dtype=jnp.int32))
    return result.reshape(lag_count, second_set.shape[1], first_set.shape[1])


def on_device(traces, valid):
    length = traces.shape[2]
    dft_table, cosines, sines = make_tables(length, MAXLAG)
    whitened = whiten(traces, valid, dft_table)
    first_set = lax.all_gather(whitened, "col", axis=1, tiled=True)
    second_set = lax.all_gather(whitened, "row", axis=1, tiled=True)
    groups_row = lax.axis_size("row")
    seg_count = lax.axis_size("seg")
    segments_all = whitened.shape[0] * seg_count
    scale = 1.0 / math.sqrt(segments_all * (length // 2))
    own_count = whitened.shape[1]
    partial_value = lag_sums(first_set, second_set, cosines, sines, LAGSET)
    partial_value = partial_value.reshape(
        partial_value.shape[0], groups_row, own_count, partial_value.shape[2]
    )
    summed = lax.psum_scatter(partial_value, "seg", scatter_dimension=2, tiled=True)
    return summed * scale


def solution(mesh):
    placed = (P("seg", ("row", "col"), None), P("seg", ("row", "col")))
    return jax.shard_map(
        on_device,
        mesh=mesh,
        in_specs=placed,
        out_specs=P(None, None, ("col", "seg"), "row"),
        check_vma=False,
    )
```

profile of v0, /device:TPU:0, one launch (start us, length us, event | category | flops | bytes accessed | tf_op | source)
XLA Modules:
  0.0 119.5 jit_solution(4100799459907360552)
XLA Ops:
  6.5 8.5 %negate_convert_fusion = (bf16[1024,512]{1,0:T(8,128)(2,1)S(1)}, bf16[1024,512]{1,0:T(8,128)(2,1)S(1)}) fusion(), kind=kLoop, calls=%fused_computation.21 | loop fusion | flops 8912896 | bytes 2097152 | tf_op jit(solution)/shard_map/convert.5
  15.9 0.6 pad_maximum_fusion
  17.0 40.3 %all-gather.2.cloned.1.call-done = bf16[4,128,1024]{2,1,0:T(8,128)(2,1)} async-done(((bf16[4,8,1024]{2,1,0:T(8,128)(2,1)}), bf16[4,128,1024]{2,1,0:T(8,128)(2,1)}) %all-gather.2.cloned.1.call-update) | async-done | bytes 1048592 | tf_op jit(solution)/shard_map/all_gather | solution.py:61
  57.3 32.3 %while.10 = (s32[]{:T(128)}, f32[11,3,8,128]{3,2,1,0:T(8,128)S(1)}, f32[4,8,512]{2,1,0:T(8,128)S(1)}, s32[11]{0:T(128)S(1)}, f32[33,512]{1,0:T(8,128)S(1)}, /*in...) while((s32[]{:T(128)}, f32[11,3,8,128]{3,2,1,0:T(8,128)S(1)}, ...), condition=%wide.region_2.3_spmd, body=%wide.region_1.2_spmd.sunk | while | flops 25952260 | bytes 1622199 | solution.py:53
  58.6 1.6 %fusion.37 = f32[11,3,8,128]{3,2,1,0:T(8,128)S(1)} fusion(f32[11,3,8,128]{3,2,1,0:T(8,128)S(1)} %get-tuple-element.148, s32[]{:T(128)} %get-tuple-element.147, bf16[4,128,1024]{2,1,0:T(8,128)(2,1)} %get-tuple-element.166, bf16[3,4,8,512]{3,2,1,0:T(8,128)(2,1)S(1)} %get-tuple-element.133, bf16[3,4,8,512]{3,2,1,0:T(8,128)(2,1)S(1)} %get-tuple-element.134), kind=kOutput, calls=%fused_computation.1.clone.1 | convolution fusion | flops 25559040 | bytes 1257476 | tf_op jit(solution)/shard_map/while/body/eval_jaxpr/gsbk,sak->gba/dot_general | solution.py:51
  60.2 0.6 dynamic_slice.15
  61.5 1.6 %fusion.37 = f32[11,3,8,128]{3,2,1,0:T(8,128)S(1)} fusion(f32[11,3,8,128]{3,2,1,0:T(8,128)S(1)} %get-tuple-element.148, s32[]{:T(128)} %get-tuple-element.147, bf16[4,128,1024]{2,1,0:T(8,128)(2,1)} %get-tuple-element.166, bf16[3,4,8,512]{3,2,1,0:T(8,128)(2,1)S(1)} %get-tuple-element.133, bf16[3,4,8,512]{3,2,1,0:T(8,128)(2,1)S(1)} %get-tuple-element.134), kind=kOutput, calls=%fused_computation.1.clone.1 | convolution fusion | flops 25559040 | bytes 1257476 | tf_op jit(solution)/shard_map/while/body/eval_jaxpr/gsbk,sak->gba/dot_general | solution.py:51
  63.2 0.6 dynamic_slice.15
  64.5 1.6 %fusion.37 = f32[11,3,8,128]{3,2,1,0:T(8,128)S(1)} fusion(f32[11,3,8,128]{3,2,1,0:T(8,128)S(1)} %get-tuple-element.148, s32[]{:T(128)} %get-tuple-element.147, bf16[4,128,1024]{2,1,0:T(8,128)(2,1)} %get-tuple-element.166, bf16[3,4,8,512]{3,2,1,0:T(8,128)(2,1)S(1)} %get-tuple-element.133, bf16[3,4,8,512]{3,2,1,0:T(8,128)(2,1)S(1)} %get-tuple-element.134), kind=kOutput, calls=%fused_computation.1.clone.1 | convolution fusion | flops 25559040 | bytes 1257476 | tf_op jit(solution)/shard_map/while/body/eval_jaxpr/gsbk,sak->gba/dot_general | solution.py:51
  66.1 0.6 dynamic_slice.15
  67.4 1.6 %fusion.37 = f32[11,3,8,128]{3,2,1,0:T(8,128)S(1)} fusion(f32[11,3,8,128]{3,2,1,0:T(8,128)S(1)} %get-tuple-element.148, s32[]{:T(128)} %get-tuple-element.147, bf16[4,128,1024]{2,1,0:T(8,128)(2,1)} %get-tuple-element.166, bf16[3,4,8,512]{3,2,1,0:T(8,128)(2,1)S(1)} %get-tuple-element.133, bf16[3,4,8,512]{3,2,1,0:T(8,128)(2,1)S(1)} %get-tuple-element.134), kind=kOutput, calls=%fused_computation.1.clone.1 | convolution fusion | flops 25559040 | bytes 1257476 | tf_op jit(solution)/shard_map/while/body/eval_jaxpr/gsbk,sak->gba/dot_general | solution.py:51
  69.0 0.6 dynamic_slice.15
  70.4 1.6 %fusion.37 = f32[11,3,8,128]{3,2,1,0:T(8,128)S(1)} fusion(f32[11,3,8,128]{3,2,1,0:T(8,128)S(1)} %get-tuple-element.148, s32[]{:T(128)} %get-tuple-element.147, bf16[4,128,1024]{2,1,0:T(8,128)(2,1)} %get-tuple-element.166, bf16[3,4,8,512]{3,2,1,0:T(8,128)(2,1)S(1)} %get-tuple-element.133, bf16[3,4,8,512]{3,2,1,0:T(8,128)(2,1)S(1)} %get-tuple-element.134), kind=kOutput, calls=%fused_computation.1.clone.1 | convolution fusion | flops 25559040 | bytes 1257476 | tf_op jit(solution)/shard_map/while/body/eval_jaxpr/gsbk,sak->gba/dot_general | solution.py:51
  72.0 0.6 dynamic_slice.15
  73.3 1.6 %fusion.37 = f32[11,3,8,128]{3,2,1,0:T(8,128)S(1)} fusion(f32[11,3,8,128]{3,2,1,0:T(8,128)S(1)} %get-tuple-element.148, s32[]{:T(128)} %get-tuple-element.147, bf16[4,128,1024]{2,1,0:T(8,128)(2,1)} %get-tuple-element.166, bf16[3,4,8,512]{3,2,1,0:T(8,128)(2,1)S(1)} %get-tuple-element.133, bf16[3,4,8,512]{3,2,1,0:T(8,128)(2,1)S(1)} %get-tuple-element.134), kind=kOutput, calls=%fused_computation.1.clone.1 | convolution fusion | flops 25559040 | bytes 1257476 | tf_op jit(solution)/shard_map/while/body/eval_jaxpr/gsbk,sak->gba/dot_general | solution.py:51
  74.9 0.6 dynamic_slice.15
  76.3 1.6 %fusion.37 = f32[11,3,8,128]{3,2,1,0:T(8,128)S(1)} fusion(f32[11,3,8,128]{3,2,1,0:T(8,128)S(1)} %get-tuple-element.148, s32[]{:T(128)} %get-tuple-element.147, bf16[4,128,1024]{2,1,0:T(8,128)(2,1)} %get-tuple-element.166, bf16[3,4,8,512]{3,2,1,0:T(8,128)(2,1)S(1)} %get-tuple-element.133, bf16[3,4,8,512]{3,2,1,0:T(8,128)(2,1)S(1)} %get-tuple-element.134), kind=kOutput, calls=%fused_computation.1.clone.1 | convolution fusion | flops 25559040 | bytes 1257476 | tf_op jit(solution)/shard_map/while/body/eval_jaxpr/gsbk,sak->gba/dot_general | solution.py:51
  79.2 1.6 %fusion.37 = f32[11,3,8,128]{3,2,1,0:T(8,128)S(1)} fusion(f32[11,3,8,128]{3,2,1,0:T(8,128)S(1)} %get-tuple-element.148, s32[]{:T(128)} %get-tuple-element.147, bf16[4,128,1024]{2,1,0:T(8,128)(2,1)} %get-tuple-element.166, bf16[3,4,8,512]{3,2,1,0:T(8,128)(2,1)S(1)} %get-tuple-element.133, bf16[3,4,8,512]{3,2,1,0:T(8,128)(2,1)S(1)} %get-tuple-element.134), kind=kOutput, calls=%fused_computation.1.clone.1 | convolution fusion | flops 25559040 | bytes 1257476 | tf_op jit(solution)/shard_map/while/body/eval_jaxpr/gsbk,sak->gba/dot_general | solution.py:51
  82.1 1.6 %fusion.37 = f32[11,3,8,128]{3,2,1,0:T(8,128)S(1)} fusion(f32[11,3,8,128]{3,2,1,0:T(8,128)S(1)} %get-tuple-element.148, s32[]{:T(128)} %get-tuple-element.147, bf16[4,128,1024]{2,1,0:T(8,128)(2,1)} %get-tuple-element.166, bf16[3,4,8,512]{3,2,1,0:T(8,128)(2,1)S(1)} %get-tuple-element.133, bf16[3,4,8,512]{3,2,1,0:T(8,128)(2,1)S(1)} %get-tuple-element.134), kind=kOutput, calls=%fused_computation.1.clone.1 | convolution fusion | flops 25559040 | bytes 1257476 | tf_op jit(solution)/shard_map/while/body/eval_jaxpr/gsbk,sak->gba/dot_general | solution.py:51
  85.1 1.6 %fusion.37 = f32[11,3,8,128]{3,2,1,0:T(8,128)S(1)} fusion(f32[11,3,8,128]{3,2,1,0:T(8,128)S(1)} %get-tuple-element.148, s32[]{:T(128)} %get-tuple-element.147, bf16[4,128,1024]{2,1,0:T(8,128)(2,1)} %get-tuple-element.166, bf16[3,4,8,512]{3,2,1,0:T(8,128)(2,1)S(1)} %get-tuple-element.133, bf16[3,4,8,512]{3,2,1,0:T(8,128)(2,1)S(1)} %get-tuple-element.134), kind=kOutput, calls=%fused_computation.1.clone.1 | convolution fusion | flops 25559040 | bytes 1257476 | tf_op jit(solution)/shard_map/while/body/eval_jaxpr/gsbk,sak->gba/dot_general | solution.py:51
  88.0 1.6 %fusion.37 = f32[11,3,8,128]{3,2,1,0:T(8,128)S(1)} fusion(f32[11,3,8,128]{3,2,1,0:T(8,128)S(1)} %get-tuple-element.148, s32[]{:T(128)} %get-tuple-element.147, bf16[4,128,1024]{2,1,0:T(8,128)(2,1)} %get-tuple-element.166, bf16[3,4,8,512]{3,2,1,0:T(8,128)(2,1)S(1)} %get-tuple-element.133, bf16[3,4,8,512]{3,2,1,0:T(8,128)(2,1)S(1)} %get-tuple-element.134), kind=kOutput, calls=%fused_computation.1.clone.1 | convolution fusion | flops 25559040 | bytes 1257476 | tf_op jit(solution)/shard_map/while/body/eval_jaxpr/gsbk,sak->gba/dot_general | solution.py:51
  89.6 0.6 copy-done.1
  91.6 19.5 %all-reduce.3.cloned.1.call-done = f32[33,1,8,128]{3,2,1,0:T(8,128)} async-done(((f32[33,1,8,128]{3,2,1,0:T(8,128)}), f32[33,1,8,128]{3,2,1,0:T(8,128)}) %all-reduce.3.cloned.1.call-update) | async-done | bytes 135184
  111.1 1.6 %dynamic-slice_multiply_fusion = f32[33,1,4,128]{3,2,1,0:T(4,128)} fusion(f32[33,1,8,128]{3,2,1,0:T(8,128)} %all-reduce.3.cloned.1.call-done, u32[]{:T(128)S(6)} %multiply.4), kind=kLoop, calls=%fused_computation.36 | loop fusion | flops 16896 | bytes 135172 | tf_op jit(solution)/shard_map/mul | solution.py:73
  (48 shorter events, 5.5 us)
Async XLA Ops:
  6.5 8.6 %copy-start = (bf16[4,8,1024]{2,1,0:T(8,128)(2,1)S(1)}, bf16[4,8,1024]{2,1,0:T(8,128)(2,1)}, u32[]{:S(2)}) copy-start(bf16[4,8,1024]{2,1,0:T(8,128)(2,1)} %param.4) | copy-start | bytes 196612
  6.5 50.7 %all-gather.2.cloned.1.call-start = ((), (), s32[]{:S(2)}) async-start(), calls=%async_computation | async-start | bytes 1114112 | tf_op jit(solution)/shard_map/all_gather | solution.py:61
  15.1 0.7 copy-start.2
  16.5 94.5 %all-reduce.3.cloned.1.call-start = ((), (), s32[]{:S(2)}) async-start(), calls=%async_computation.1 | async-start | bytes 270336
  57.3 33.0 %copy-start.3 = (u32[32]{0:T(128)S(1)}, u32[32]{0:T(128)}, u32[]{:S(2)}) copy-start(u32[32]{0:T(128)} %constant.59) | copy-start | bytes 388
  89.6 0.7 copy-start.1
Sparse Core Ops, SparseCore 0:
  16.7 40.5 all-gather.1
  90.4 20.5 all-reduce.2
where the time goes:
time: 120 us; the launch traced here: 119 us
  waiting for transfers between devices  59.8 us (50%)
  matrix products  18.1 us (15%)
  between operations  14.1 us (12%)
  other arithmetic  11.9 us (10%)
  local copies, waits for them, and re-layouts  8.06 us (7%)
  loops' own time  7.39 us (6%)
    all_gather x1, waiting for transfers between devices, on_device(): first_set = lax.all_gather(whitened, 'col', axis=1, tiled=True)  40.3 us
    unnamed x3, waiting for transfers between devices  19.5 us
    dot_general x11, matrix products, one_group(): jnp.einsum('gsbk,sak->gba', rotated, first_set, preferred_element_type=jn...  17.7 us
    another operation x12, other arithmetic  9.11 us
    another operation x1, loops' own time, lag_sums(): lax.map(one_group, jnp.arange(lag_count // group_size, dtype=jnp.int32))  7.39 us
    dynamic_slice x11, local copies, waits for them, and re-layouts, lag_sums(): lax.map(one_group, jnp.arange(lag_count // group_size, dtype=jnp.int32))  6.54 us
  transfers between devices with their start and end apart: 2, of which 2 were waited for; matrix products, arithmetic and copies ran while one was open for 1% of the time, Pallas kernels for 0%

commit v1 on v0

--- a/solution.py
+++ b/solution.py
@@ -6,6 +6,24 @@
 
 MAXLAG = 16
 LAGSET = 3
+
+
+def ring_gather(array, axis, dim):
+    ways, here, hop = (lax.axis_size(axis), lax.axis_index(axis), array.shape[dim])
+    shape = [n * ways if d == dim else n for d, n in enumerate(array.shape)]
+    full = lax.dynamic_update_slice_in_dim(
+        jnp.zeros(shape, array.dtype), array, here * hop, axis=dim
+    )
+    going_up = going_down = array
+    for far in range(1, ways // 2 + 1):
+        going_up = lax.ppermute(going_up, axis, [(d, (d + 1) % ways) for d in range(ways)])
+        full = lax.dynamic_update_slice_in_dim(full, going_up, (here - far) % ways * hop, axis=dim)
+        if 2 * far < ways:
+            going_down = lax.ppermute(going_down, axis, [(d, (d - 1) % ways) for d in range(ways)])
+            full = lax.dynamic_update_slice_in_dim(
+                full, going_down, (here + far) % ways * hop, axis=dim
+            )
+    return full
 
 
 def make_tables(length, max_shift):
@@ -58,7 +76,7 @@
     length = traces.shape[2]
     dft_table, cosines, sines = make_tables(length, MAXLAG)
     whitened = whiten(traces, valid, dft_table)
-    first_set = lax.all_gather(whitened, "col", axis=1, tiled=True)
+    first_set = ring_gather(whitened, "col", 1)
     second_set = lax.all_gather(whitened, "row", axis=1, tiled=True)
     groups_row = lax.axis_size("row")
     seg_count = lax.axis_size("seg")

time: 120 us -> 116 us (0.967)
  starting transfers between devices: 0.04 us -> 32.4 us
  waiting for transfers between devices: 59.8 us -> 37 us
  matrix products: 18.1 us -> 4.69 us
    all_gather x1 -> x0, waiting for transfers between devices: 40.3 us -> none  [on_device(): first_set = lax.all_gather(whitened, 'col', axis=1, tiled=True)]
    ppermute x0 -> x15, starting transfers between devices: none -> 32.4 us  [the longest x7 31.9 us: ring_gather(): lax.ppermute(going_down, axis, [(d, (d - 1) % ways) for d in range(ways)])]
    ppermute x0 -> x15, waiting for transfers between devices: none -> 18.9 us  [the longest x8 18.8 us: ring_gather(): lax.ppermute(going_up, axis, [(d, (d + 1) % ways) for d in range(ways)])]
    dot_general x11, matrix products: 17.7 us -> 4.24 us  [one_group(): jnp.einsum('gsbk,sak->gba', rotated, first_set, preferred_element_type=jn...]
    unnamed x3 -> x2, waiting for transfers between devices: 19.5 us -> 18.1 us
  transfers between devices with their start and end apart: 2 -> 16, of which waited for: 2 -> 9; matrix products, arithmetic and copies ran while one was open for 1% -> 1% of each run, Pallas kernels for 0% -> 0%
where the time goes in v1:
time: 116 us
  waiting for transfers between devices  37 us (32%)
  starting transfers between devices  32.4 us (28%)
  between operations  14.6 us (13%)
  other arithmetic  11.3 us (10%)
  local copies, waits for them, and re-layouts  9 us (8%)
  loops' own time  7.14 us (6%)
  matrix products  4.69 us (4%)
    ppermute x7, starting transfers between devices, ring_gather(): lax.ppermute(going_down, axis, [(d, (d - 1) % ways) for d in range(ways)])  31.9 us
    ppermute x8, waiting for transfers between devices, ring_gather(): lax.ppermute(going_up, axis, [(d, (d + 1) % ways) for d in range(ways)])  18.8 us
    unnamed x2, waiting for transfers between devices  18.1 us
    another operation x12, other arithmetic  9.11 us
    dynamic_slice x11, local copies, waits for them, and re-layouts, lag_sums(): lax.map(one_group, jnp.arange(lag_count // group_size, dtype=jnp.int32))  7.21 us
    another operation x1, loops' own time, lag_sums(): lax.map(one_group, jnp.arange(lag_count // group_size, dtype=jnp.int32))  7.14 us
    dot_general x11, matrix products, one_group(): jnp.einsum('gsbk,sak->gba', rotated, first_set, preferred_element_type=jn...  4.24 us
  transfers between devices with their start and end apart: 16, of which 9 were waited for; matrix products, arithmetic and copies ran while one was open for 1% of the time, Pallas kernels for 0%

profile of v1, /device:TPU:0, one launch (start us, length us, event | category | flops | bytes accessed | tf_op | source)
XLA Modules:
  0.0 116.1 jit_solution(4058628714386787145)
XLA Ops:
  6.5 8.5 %negate_convert_fusion = (bf16[1024,512]{1,0:T(8,128)(2,1)S(1)}, bf16[1024,512]{1,0:T(8,128)(2,1)S(1)}) fusion(), kind=kLoop, calls=%fused_computation.21 | loop fusion | flops 8912896 | bytes 2097152 | tf_op jit(solution)/shard_map/convert.5
  16.6 5.0 %collective-permute-start.1 = (bf16[4,8,1024]{2,1,0:T(8,128)(2,1)S(1)}, bf16[4,8,1024]{2,1,0:T(8,128)(2,1)S(1)}, u32[]{:S(2)}, u32[]{:S(2)}) collective-permute-start(bf16[4,8,1024]{2,1,0:T(8,128)(2,1)S(1)} %get-tuple-element.74), channel_id=1, source_target_pairs={{0,30},{2,0},{4,2},{6,4},{8,6},{10,8},{12,10},{14,12},{16,14},{18,... | collective-permute-start | bytes 196616 | tf_op jit(solution)/shard_map/ppermute | solution.py:22
  22.4 1.2 %collective-permute-done = bf16[4,8,1024]{2,1,0:T(8,128)(2,1)S(1)} collective-permute-done((bf16[4,8,1024]{2,1,0:T(8,128)(2,1)S(1)}, bf16[4,8,1024]{2,1,0:T(8,128)(2,1)S(1)}, u32[]{:S(2)}, u32[]{:S(2)}) %collective-permute-start) | collective-permute-done | bytes 65568 | tf_op jit(solution)/shard_map/ppermute | solution.py:19
  23.6 4.4 %collective-permute-start.3 = (bf16[4,8,1024]{2,1,0:T(8,128)(2,1)S(1)}, bf16[4,8,1024]{2,1,0:T(8,128)(2,1)S(1)}, u32[]{:S(2)}, u32[]{:S(2)}) collective-permute-start(bf16[4,8,1024]{2,1,0:T(8,128)(2,1)S(1)} %collective-permute-done.1), channel_id=1, source_target_pairs={{0,30},{2,0},{4,2},{6,4},{8,6},{10,8},{12,10},{14,12},{16,14},{18,... | collective-permute-start | bytes 196616 | tf_op jit(solution)/shard_map/ppermute | solution.py:22
  28.1 1.9 %collective-permute-done.2 = bf16[4,8,1024]{2,1,0:T(8,128)(2,1)S(1)} collective-permute-done((bf16[4,8,1024]{2,1,0:T(8,128)(2,1)S(1)}, bf16[4,8,1024]{2,1,0:T(8,128)(2,1)S(1)}, u32[]{:S(2)}, u32[]{:S(2)}) %collective-permute-start.2) | collective-permute-done | bytes 65568 | tf_op jit(solution)/shard_map/ppermute | solution.py:19
  30.0 4.4 %collective-permute-start.5 = (bf16[4,8,1024]{2,1,0:T(8,128)(2,1)S(1)}, bf16[4,8,1024]{2,1,0:T(8,128)(2,1)S(1)}, u32[]{:S(2)}, u32[]{:S(2)}) collective-permute-start(bf16[4,8,1024]{2,1,0:T(8,128)(2,1)S(1)} %collective-permute-done.3), channel_id=1, source_target_pairs={{0,30},{2,0},{4,2},{6,4},{8,6},{10,8},{12,10},{14,12},{16,14},{18,... | collective-permute-start | bytes 196616 | tf_op jit(solution)/shard_map/ppermute | solution.py:22
  34.5 1.9 %collective-permute-done.4 = bf16[4,8,1024]{2,1,0:T(8,128)(2,1)S(1)} collective-permute-done((bf16[4,8,1024]{2,1,0:T(8,128)(2,1)S(1)}, bf16[4,8,1024]{2,1,0:T(8,128)(2,1)S(1)}, u32[]{:S(2)}, u32[]{:S(2)}) %collective-permute-start.4) | collective-permute-done | bytes 65568 | tf_op jit(solution)/shard_map/ppermute | solution.py:19
  36.4 4.5 %collective-permute-start.7 = (bf16[4,8,1024]{2,1,0:T(8,128)(2,1)S(1)}, bf16[4,8,1024]{2,1,0:T(8,128)(2,1)S(1)}, u32[]{:S(2)}, u32[]{:S(2)}) collective-permute-start(bf16[4,8,1024]{2,1,0:T(8,128)(2,1)S(1)} %collective-permute-done.5), channel_id=1, source_target_pairs={{0,30},{2,0},{4,2},{6,4},{8,6},{10,8},{12,10},{14,12},{16,14},{18,... | collective-permute-start | bytes 196616 | tf_op jit(solution)/shard_map/ppermute | solution.py:22
  40.9 1.9 %collective-permute-done.6 = bf16[4,8,1024]{2,1,0:T(8,128)(2,1)S(1)} collective-permute-done((bf16[4,8,1024]{2,1,0:T(8,128)(2,1)S(1)}, bf16[4,8,1024]{2,1,0:T(8,128)(2,1)S(1)}, u32[]{:S(2)}, u32[]{:S(2)}) %collective-permute-start.6) | collective-permute-done | bytes 65568 | tf_op jit(solution)/shard_map/ppermute | solution.py:19
  42.8 4.5 %collective-permute-start.9 = (bf16[4,8,1024]{2,1,0:T(8,128)(2,1)S(1)}, bf16[4,8,1024]{2,1,0:T(8,128)(2,1)S(1)}, u32[]{:S(2)}, u32[]{:S(2)}) collective-permute-start(bf16[4,8,1024]{2,1,0:T(8,128)(2,1)S(1)} %collective-permute-done.7), channel_id=1, source_target_pairs={{0,30},{2,0},{4,2},{6,4},{8,6},{10,8},{12,10},{14,12},{16,14},{18,... | collective-permute-start | bytes 196616 | tf_op jit(solution)/shard_map/ppermute | solution.py:22
  47.3 1.9 %collective-permute-done.8 = bf16[4,8,1024]{2,1,0:T(8,128)(2,1)S(1)} collective-permute-done((bf16[4,8,1024]{2,1,0:T(8,128)(2,1)S(1)}, bf16[4,8,1024]{2,1,0:T(8,128)(2,1)S(1)}, u32[]{:S(2)}, u32[]{:S(2)}) %collective-permute-start.8) | collective-permute-done | bytes 65568 | tf_op jit(solution)/shard_map/ppermute | solution.py:19
  49.2 4.5 %collective-permute-start.11 = (bf16[4,8,1024]{2,1,0:T(8,128)(2,1)S(1)}, bf16[4,8,1024]{2,1,0:T(8,128)(2,1)S(1)}, u32[]{:S(2)}, u32[]{:S(2)}) collective-permute-start(bf16[4,8,1024]{2,1,0:T(8,128)(2,1)S(1)} %collective-permute-done.9), channel_id=1, source_target_pairs={{0,30},{2,0},{4,2},{6,4},{8,6},{10,8},{12,10},{14,12},{16,14},{18,... | collective-permute-start | bytes 196616 | tf_op jit(solution)/shard_map/ppermute | solution.py:22
  53.7 1.9 %collective-permute-done.10 = bf16[4,8,1024]{2,1,0:T(8,128)(2,1)S(1)} collective-permute-done((bf16[4,8,1024]{2,1,0:T(8,128)(2,1)S(1)}, bf16[4,8,1024]{2,1,0:T(8,128)(2,1)S(1)}, u32[]{:S(2)}, u32[]{:S(2)}) %collective-permute-start.10) | collective-permute-done | bytes 65568 | tf_op jit(solution)/shard_map/ppermute | solution.py:19
  55.6 4.5 %collective-permute-start.13 = (bf16[4,8,1024]{2,1,0:T(8,128)(2,1)S(1)}, bf16[4,8,1024]{2,1,0:T(8,128)(2,1)S(1)}, u32[]{:S(2)}, u32[]{:S(2)}) collective-permute-start(bf16[4,8,1024]{2,1,0:T(8,128)(2,1)S(1)} %collective-permute-done.11), channel_id=1, source_target_pairs={{0,30},{2,0},{4,2},{6,4},{8,6},{10,8},{12,10},{14,12},{16,14},{18,... | collective-permute-start | bytes 196616 | tf_op jit(solution)/shard_map/ppermute | solution.py:22
  60.1 1.9 %collective-permute-done.12 = bf16[4,8,1024]{2,1,0:T(8,128)(2,1)S(1)} collective-permute-done((bf16[4,8,1024]{2,1,0:T(8,128)(2,1)S(1)}, bf16[4,8,1024]{2,1,0:T(8,128)(2,1)S(1)}, u32[]{:S(2)}, u32[]{:S(2)}) %collective-permute-start.12) | collective-permute-done | bytes 65568 | tf_op jit(solution)/shard_map/ppermute | solution.py:19
  62.0 6.3 %collective-permute-done.14 = bf16[4,8,1024]{2,1,0:T(8,128)(2,1)S(1)} collective-permute-done((bf16[4,8,1024]{2,1,0:T(8,128)(2,1)S(1)}, bf16[4,8,1024]{2,1,0:T(8,128)(2,1)S(1)}, u32[]{:S(2)}, u32[]{:S(2)}) %collective-permute-start.14) | collective-permute-done | bytes 65568 | tf_op jit(solution)/shard_map/ppermute | solution.py:19
  68.4 19.3 %while.10 = (s32[]{:T(128)}, f32[11,3,8,128]{3,2,1,0:T(8,128)S(1)}, f32[4,8,512]{2,1,0:T(8,128)S(1)}, s32[11]{0:T(128)S(1)}, f32[33,512]{1,0:T(8,128)S(1)}, /*in...) while((s32[]{:T(128)}, f32[11,3,8,128]{3,2,1,0:T(8,128)S(1)}, ...), condition=%wide.region_2.3_spmd, body=%wide.region_1.2_spmd.sunk | while | flops 25952260 | bytes 1622199 | solution.py:71
  70.1 0.7 dynamic_slice.15
  75.4 0.7 dynamic_slice.15
  80.7 0.7 dynamic_slice.15
  82.4 0.7 dynamic_slice.15
  84.2 0.7 dynamic_slice.15
  89.6 18.1 %all-reduce.3.cloned.1.call-done = f32[33,1,8,128]{3,2,1,0:T(8,128)} async-done(((f32[33,1,8,128]{3,2,1,0:T(8,128)}), f32[33,1,8,128]{3,2,1,0:T(8,128)}) %all-reduce.3.cloned.1.call-update) | async-done | bytes 135184
  107.7 1.6 %dynamic-slice_multiply_fusion = f32[33,1,4,128]{3,2,1,0:T(4,128)} fusion(f32[33,1,8,128]{3,2,1,0:T(8,128)} %all-reduce.3.cloned.1.call-done, u32[]{:T(128)S(6)} %multiply.4), kind=kLoop, calls=%fused_computation.36 | loop fusion | flops 16896 | bytes 135172 | tf_op jit(solution)/shard_map/mul | solution.py:91
  (91 shorter events, 12.2 us)
Async XLA Ops:
  6.5 8.6 %copy-start = (bf16[4,8,1024]{2,1,0:T(8,128)(2,1)S(1)}, bf16[4,8,1024]{2,1,0:T(8,128)(2,1)}, u32[]{:S(2)}) copy-start(bf16[4,8,1024]{2,1,0:T(8,128)(2,1)} %param.4) | copy-start | bytes 196612
  6.5 101.2 %all-reduce.3.cloned.1.call-start = ((), (), s32[]{:S(2)}) async-start(), calls=%async_computation | async-start | bytes 270336
  15.1 0.7 copy-start.2
  16.0 7.6 %collective-permute-start = (bf16[4,8,1024]{2,1,0:T(8,128)(2,1)S(1)}, bf16[4,8,1024]{2,1,0:T(8,128)(2,1)S(1)}, u32[]{:S(2)}, u32[]{:S(2)}) collective-permute-start(bf16[4,8,1024]{2,1,0:T(8,128)(2,1)S(1)} %get-tuple-element.74), channel_id=1, source_target_pairs={{0,2},{2,4},{4,6},{6,8},{8,10},{10,12},{12,14},{14,16},{16,18},{18... | collective-permute-start | bytes 196616 | tf_op jit(solution)/shard_map/ppermute | solution.py:19
  16.6 7.0 %collective-permute-start.1 = (bf16[4,8,1024]{2,1,0:T(8,128)(2,1)S(1)}, bf16[4,8,1024]{2,1,0:T(8,128)(2,1)S(1)}, u32[]{:S(2)}, u32[]{:S(2)}) collective-permute-start(bf16[4,8,1024]{2,1,0:T(8,128)(2,1)S(1)} %get-tuple-element.74), channel_id=1, source_target_pairs={{0,30},{2,0},{4,2},{6,4},{8,6},{10,8},{12,10},{14,12},{16,14},{18,... | collective-permute-start | bytes 196616 | tf_op jit(solution)/shard_map/ppermute | solution.py:22
  23.6 6.4 %collective-permute-start.2 = (bf16[4,8,1024]{2,1,0:T(8,128)(2,1)S(1)}, bf16[4,8,1024]{2,1,0:T(8,128)(2,1)S(1)}, u32[]{:S(2)}, u32[]{:S(2)}) collective-permute-start(bf16[4,8,1024]{2,1,0:T(8,128)(2,1)S(1)} %collective-permute-done), channel_id=1, source_target_pairs={{0,2},{2,4},{4,6},{6,8},{8,10},{10,12},{12,14},{14,16},{16,18},{18... | collective-permute-start | bytes 196616 | tf_op jit(solution)/shard_map/ppermute | solution.py:19
  23.6 6.4 %collective-permute-start.3 = (bf16[4,8,1024]{2,1,0:T(8,128)(2,1)S(1)}, bf16[4,8,1024]{2,1,0:T(8,128)(2,1)S(1)}, u32[]{:S(2)}, u32[]{:S(2)}) collective-permute-start(bf16[4,8,1024]{2,1,0:T(8,128)(2,1)S(1)} %collective-permute-done.1), channel_id=1, source_target_pairs={{0,30},{2,0},{4,2},{6,4},{8,6},{10,8},{12,10},{14,12},{16,14},{18,... | collective-permute-start | bytes 196616 | tf_op jit(solution)/shard_map/ppermute | solution.py:22
  30.0 6.4 %collective-permute-start.4 = (bf16[4,8,1024]{2,1,0:T(8,128)(2,1)S(1)}, bf16[4,8,1024]{2,1,0:T(8,128)(2,1)S(1)}, u32[]{:S(2)}, u32[]{:S(2)}) collective-permute-start(bf16[4,8,1024]{2,1,0:T(8,128)(2,1)S(1)} %collective-permute-done.2), channel_id=1, source_target_pairs={{0,2},{2,4},{4,6},{6,8},{8,10},{10,12},{12,14},{14,16},{16,18},{18... | collective-permute-start | bytes 196616 | tf_op jit(solution)/shard_map/ppermute | solution.py:19
  30.0 6.4 %collective-permute-start.5 = (bf16[4,8,1024]{2,1,0:T(8,128)(2,1)S(1)}, bf16[4,8,1024]{2,1,0:T(8,128)(2,1)S(1)}, u32[]{:S(2)}, u32[]{:S(2)}) collective-permute-start(bf16[4,8,1024]{2,1,0:T(8,128)(2,1)S(1)} %collective-permute-done.3), channel_id=1, source_target_pairs={{0,30},{2,0},{4,2},{6,4},{8,6},{10,8},{12,10},{14,12},{16,14},{18,... | collective-permute-start | bytes 196616 | tf_op jit(solution)/shard_map/ppermute | solution.py:22
  36.4 6.4 %collective-permute-start.6 = (bf16[4,8,1024]{2,1,0:T(8,128)(2,1)S(1)}, bf16[4,8,1024]{2,1,0:T(8,128)(2,1)S(1)}, u32[]{:S(2)}, u32[]{:S(2)}) collective-permute-start(bf16[4,8,1024]{2,1,0:T(8,128)(2,1)S(1)} %collective-permute-done.4), channel_id=1, source_target_pairs={{0,2},{2,4},{4,6},{6,8},{8,10},{10,12},{12,14},{14,16},{16,18},{18... | collective-permute-start | bytes 196616 | tf_op jit(solution)/shard_map/ppermute | solution.py:19
  36.4 6.4 %collective-permute-start.7 = (bf16[4,8,1024]{2,1,0:T(8,128)(2,1)S(1)}, bf16[4,8,1024]{2,1,0:T(8,128)(2,1)S(1)}, u32[]{:S(2)}, u32[]{:S(2)}) collective-permute-start(bf16[4,8,1024]{2,1,0:T(8,128)(2,1)S(1)} %collective-permute-done.5), channel_id=1, source_target_pairs={{0,30},{2,0},{4,2},{6,4},{8,6},{10,8},{12,10},{14,12},{16,14},{18,... | collective-permute-start | bytes 196616 | tf_op jit(solution)/shard_map/ppermute | solution.py:22
  42.8 6.4 %collective-permute-start.8 = (bf16[4,8,1024]{2,1,0:T(8,128)(2,1)S(1)}, bf16[4,8,1024]{2,1,0:T(8,128)(2,1)S(1)}, u32[]{:S(2)}, u32[]{:S(2)}) collective-permute-start(bf16[4,8,1024]{2,1,0:T(8,128)(2,1)S(1)} %collective-permute-done.6), channel_id=1, source_target_pairs={{0,2},{2,4},{4,6},{6,8},{8,10},{10,12},{12,14},{14,16},{16,18},{18... | collective-permute-start | bytes 196616 | tf_op jit(solution)/shard_map/ppermute | solution.py:19
  42.8 6.4 %collective-permute-start.9 = (bf16[4,8,1024]{2,1,0:T(8,128)(2,1)S(1)}, bf16[4,8,1024]{2,1,0:T(8,128)(2,1)S(1)}, u32[]{:S(2)}, u32[]{:S(2)}) collective-permute-start(bf16[4,8,1024]{2,1,0:T(8,128)(2,1)S(1)} %collective-permute-done.7), channel_id=1, source_target_pairs={{0,30},{2,0},{4,2},{6,4},{8,6},{10,8},{12,10},{14,12},{16,14},{18,... | collective-permute-start | bytes 196616 | tf_op jit(solution)/shard_map/ppermute | solution.py:22
  49.2 6.4 %collective-permute-start.10 = (bf16[4,8,1024]{2,1,0:T(8,128)(2,1)S(1)}, bf16[4,8,1024]{2,1,0:T(8,128)(2,1)S(1)}, u32[]{:S(2)}, u32[]{:S(2)}) collective-permute-start(bf16[4,8,1024]{2,1,0:T(8,128)(2,1)S(1)} %collective-permute-done.8), channel_id=1, source_target_pairs={{0,2},{2,4},{4,6},{6,8},{8,10},{10,12},{12,14},{14,16},{16,18},{18... | collective-permute-start | bytes 196616 | tf_op jit(solution)/shard_map/ppermute | solution.py:19
  49.2 6.4 %collective-permute-start.11 = (bf16[4,8,1024]{2,1,0:T(8,128)(2,1)S(1)}, bf16[4,8,1024]{2,1,0:T(8,128)(2,1)S(1)}, u32[]{:S(2)}, u32[]{:S(2)}) collective-permute-start(bf16[4,8,1024]{2,1,0:T(8,128)(2,1)S(1)} %collective-permute-done.9), channel_id=1, source_target_pairs={{0,30},{2,0},{4,2},{6,4},{8,6},{10,8},{12,10},{14,12},{16,14},{18,... | collective-permute-start | bytes 196616 | tf_op jit(solution)/shard_map/ppermute | solution.py:22
  55.6 6.4 %collective-permute-start.12 = (bf16[4,8,1024]{2,1,0:T(8,128)(2,1)S(1)}, bf16[4,8,1024]{2,1,0:T(8,128)(2,1)S(1)}, u32[]{:S(2)}, u32[]{:S(2)}) collective-permute-start(bf16[4,8,1024]{2,1,0:T(8,128)(2,1)S(1)} %collective-permute-done.10), channel_id=1, source_target_pairs={{0,2},{2,4},{4,6},{6,8},{8,10},{10,12},{12,14},{14,16},{16,18},{18... | collective-permute-start | bytes 196616 | tf_op jit(solution)/shard_map/ppermute | solution.py:19
  55.6 6.4 %collective-permute-start.13 = (bf16[4,8,1024]{2,1,0:T(8,128)(2,1)S(1)}, bf16[4,8,1024]{2,1,0:T(8,128)(2,1)S(1)}, u32[]{:S(2)}, u32[]{:S(2)}) collective-permute-start(bf16[4,8,1024]{2,1,0:T(8,128)(2,1)S(1)} %collective-permute-done.11), channel_id=1, source_target_pairs={{0,30},{2,0},{4,2},{6,4},{8,6},{10,8},{12,10},{14,12},{16,14},{18,... | collective-permute-start | bytes 196616 | tf_op jit(solution)/shard_map/ppermute | solution.py:22
  61.9 6.4 %collective-permute-start.14 = (bf16[4,8,1024]{2,1,0:T(8,128)(2,1)S(1)}, bf16[4,8,1024]{2,1,0:T(8,128)(2,1)S(1)}, u32[]{:S(2)}, u32[]{:S(2)}) collective-permute-start(bf16[4,8,1024]{2,1,0:T(8,128)(2,1)S(1)} %collective-permute-done.12), channel_id=1, source_target_pairs={{0,2},{2,4},{4,6},{6,8},{8,10},{10,12},{12,14},{14,16},{16,18},{18... | collective-permute-start | bytes 196616 | tf_op jit(solution)/shard_map/ppermute | solution.py:19
  68.4 20.0 %copy-start.3 = (u32[32]{0:T(128)S(1)}, u32[32]{0:T(128)}, u32[]{:S(2)}) copy-start(u32[32]{0:T(128)} %constant.169) | copy-start | bytes 388
  87.7 0.7 copy-start.1
Sparse Core Ops, SparseCore 0:
  88.5 19.1 all-reduce.2
